TPU v7x, 32 devices: a whole 2x2x4 slice. The times are simulated.
32 devices in a mesh: dp: 8 (over z, y), tensor: 4 (over x, core).
Axes of the slice: x: 2, y: 2, z: 4, core: 2. Of those that a mesh axis runs over, the one named last changes fastest.
Arguments:
- layer_input_rows: bfloat16 [32768, 768], P(('dp', 'tensor')), may hold values from -6 to 6
- output_gradient: bfloat16 [32768, 768], P(('dp', 'tensor')), may hold values from -6 to 6
- query_weight: bfloat16 [768, 768], P('dp', 'tensor'), may hold values from -0.21875 to 0.21875
- key_weight: bfloat16 [768, 768], P('dp', 'tensor'), may hold values from -0.21875 to 0.21875
- value_weight: bfloat16 [768, 768], P('dp', 'tensor'), may hold values from -0.21875 to 0.21875
- output_weight: bfloat16 [768, 768], P('tensor', 'dp'), may hold values from -1.75 to 1.75
- up_weight: bfloat16 [768, 3072], P('dp', 'tensor'), may hold values from -0.21875 to 0.21875
- down_weight: bfloat16 [3072, 768], P('tensor', 'dp'), may hold values from -0.109375 to 0.109375
- query_bias_vector: float32 [768], P('tensor'), may hold values from -3 to 3
- value_bias_vector: float32 [768], P('tensor'), may hold values from -3 to 3
- output_bias_vector: float32 [768], replicated, may hold values from -5 to 5
- up_bias_vector: float32 [3072], P('tensor'), may hold values from -3 to 3
- down_bias_vector: float32 [768], replicated, may hold values from -2 to 2
- query_down_frozen: bfloat16 [768, 8], replicated, may hold values from -0.21875 to 0.21875
- value_down_frozen: bfloat16 [768, 8], replicated, may hold values from -0.21875 to 0.21875
- query_up_trained: bfloat16 [8, 768], P(None, 'tensor'), may hold values from -0.59765625 to 0.59765625
- value_up_trained: bfloat16 [8, 768], P(None, 'tensor'), may hold values from -0.59765625 to 0.59765625
- first_norm_gain: float32 [768], replicated, may hold values from 0.5 to 1.5
- first_norm_bias: float32 [768], replicated, may hold values from -2 to 2
- second_norm_gain: float32 [768], replicated, may hold values from 0.5 to 1.5
- second_norm_bias: float32 [768], replicated, may hold values from -2 to 2
- segments: int32 [32768], P('dp'), may hold values from 0 to 48, as said below
- sentence_row_mask: int32 [32768], P('dp'), may hold values from 0 to 1, as said below
Outputs:
- output: bfloat16 [32768, 768], P(('dp', 'tensor'))
- grad_input: bfloat16 [32768, 768], P(('dp', 'tensor'))
- grad_lora_query: float32 [8, 768], P(None, 'tensor')
- grad_lora_value: float32 [8, 768], P(None, 'tensor')
Inputs may be any that keep to these rules, and one draw needn't show every extreme that they name: `segments`: ids restart at 0 in every sequence of 512 rows and rise by one at each sentence boundary; sentences hold 8 to 128 rows, and the first sentence of every sequence holds exactly 128 rows; in the first sequence of all rows every later sentence holds exactly 8 rows; the padding rows at a sequence's end share one more id. `sentence_row_mask`: in each sequence of 512 rows the rows after the last sentence that ends before row 512 are 0, from 1 to 128 of them; all others are 1.
All inputs are finite; a program needn't handle non-finite values.
Results may differ from a plain program's by a relative error of at most 0.02.
Values may be sent and summed in bfloat16 or wider, within the bound.
A program may use at most 128 MiB of HBM per device.

v0:
```python
import jax
import jax.numpy as jnp
from jax import lax
from jax.sharding import PartitionSpec as P

HEAD_DIM = 64
ADAPTER_RANK = 8
ADAPTER_NUMER = 16
SEQ = 512
EPSILON = 1e-05
NEG_FILL = -1e30
WIDE = jnp.float32
NARROW = jnp.bfloat16


def layer_norm(rows, gain, shift):
    mean = jnp.mean(rows, axis=-1, keepdims=True)
    centered = rows - mean
    variance = jnp.mean(centered * centered, axis=-1, keepdims=True)
    inverse = lax.rsqrt(variance + EPSILON)
    normed = centered * inverse
    return (normed * gain + shift, normed, inverse)


def norm_back(grad, normed, inverse, gain):
    scaled = grad * gain
    centered = scaled - jnp.mean(scaled, axis=-1, keepdims=True)
    return inverse * (centered - normed * jnp.mean(scaled * normed, axis=-1, keepdims=True))


def mm(left, right):
    return jnp.dot(left, right, preferred_element_type=WIDE)


def mm_nt(left, right):
    return lax.dot_general(left, right, (((1,), (1,)), ((), ())), preferred_element_type=WIDE)


def mm_tn(left, right):
    return lax.dot_general(left, right, (((0,), (0,)), ((), ())), preferred_element_type=WIDE)


def body(
    layer_input_rows,
    output_gradient,
    query_weight,
    key_weight,
    value_weight,
    output_weight,
    up_weight,
    down_weight,
    query_bias_vector,
    value_bias_vector,
    output_bias_vector,
    up_bias_vector,
    down_bias_vector,
    query_down_frozen,
    value_down_frozen,
    query_up_trained,
    value_up_trained,
    first_norm_gain,
    first_norm_bias,
    second_norm_gain,
    second_norm_bias,
    segments,
    sentence_row_mask,
):
    adapter_scale = ADAPTER_NUMER / ADAPTER_RANK
    everyone = ("tensor", "dp")

    def spread(block):
        return lax.all_gather(block, everyone, axis=0, tiled=True)

    width = layer_input_rows.shape[1]
    rows = layer_input_rows.shape[0]

    def columns(block):
        full = spread(block)
        groups = full.shape[0] // width
        return full.reshape(groups, width, block.shape[1]).transpose(1, 0, 2).reshape(width, -1)

    full_query = columns(query_weight)
    full_key = columns(key_weight)
    full_value = columns(value_weight)
    full_out_t = columns(output_weight.T)
    full_up = columns(up_weight)
    full_down_t = columns(down_weight.T)
    query_bias = lax.all_gather(query_bias_vector, "tensor", axis=0, tiled=True)
    value_bias = lax.all_gather(value_bias_vector, "tensor", axis=0, tiled=True)
    up_bias = lax.all_gather(up_bias_vector, "tensor", axis=0, tiled=True)
    query_up = lax.all_gather(query_up_trained, "tensor", axis=1, tiled=True)
    value_up = lax.all_gather(value_up_trained, "tensor", axis=1, tiled=True)
    place = lax.axis_index("tensor")
    segment_ids = lax.dynamic_slice_in_dim(segments, place * rows, rows).reshape(-1, SEQ)
    live = lax.dynamic_slice_in_dim(sentence_row_mask, place * rows, rows).reshape(-1, SEQ)
    seqs = rows // SEQ
    heads = width // HEAD_DIM
    x = layer_input_rows
    u_q = mm(x, query_down_frozen).astype(NARROW)
    u_v = mm(x, value_down_frozen).astype(NARROW)
    q = (mm(x, full_query) + query_bias + adapter_scale * mm(u_q, query_up)).astype(NARROW)
    k = mm(x, full_key).astype(NARROW)
    v = (mm(x, full_value) + value_bias + adapter_scale * mm(u_v, value_up)).astype(NARROW)

    def by_heads(block):
        return block.reshape(seqs, SEQ, heads, HEAD_DIM)

    scale = HEAD_DIM ** (-0.5)
    qh, kh, vh = (by_heads(q), by_heads(k), by_heads(v))
    places = jnp.arange(SEQ)
    allowed = (segment_ids[:, :, None] == segment_ids[:, None, :]) & (live[:, None, :] == 1)
    allowed = allowed | (places[:, None] == places[None, :])[None]
    scores = jnp.einsum("sqhd,skhd->shqk", qh, kh, preferred_element_type=WIDE) * scale
    scores = jnp.where(allowed[:, None], scores, NEG_FILL)
    highest = jnp.max(scores, axis=-1, keepdims=True)
    powers = jnp.exp(scores - highest)
    probs = (powers / jnp.sum(powers, axis=-1, keepdims=True)).astype(NARROW)
    context = (
        jnp.einsum("shqk,skhd->sqhd", probs, vh, preferred_element_type=WIDE)
        .astype(NARROW)
        .reshape(rows, width)
    )
    attn = mm_nt(context, full_out_t) + output_bias_vector
    first, n1, s1 = layer_norm(x.astype(WIDE) + attn, first_norm_gain, first_norm_bias)
    middle = first.astype(NARROW)
    inner = mm(middle, full_up) + up_bias
    active, slope = jax.vjp(lambda value: jax.nn.gelu(value, approximate=False), inner)
    ffn = mm_nt(active.astype(NARROW), full_down_t) + down_bias_vector
    output, n2, s2 = layer_norm(first + ffn, second_norm_gain, second_norm_bias)
    grad_second = norm_back(output_gradient.astype(WIDE), n2, s2, second_norm_gain)
    grad_active = mm(grad_second.astype(NARROW), full_down_t)
    grad_inner = slope(grad_active)[0].astype(NARROW)
    grad_first = norm_back(grad_second + mm_nt(grad_inner, full_up), n1, s1, first_norm_gain)
    grad_context = by_heads(mm(grad_first.astype(NARROW), full_out_t).astype(NARROW))
    grad_probs = jnp.einsum("sqhd,skhd->shqk", grad_context, vh, preferred_element_type=WIDE)
    probs_wide = probs.astype(WIDE)
    inside = jnp.sum(probs_wide * grad_probs, axis=-1, keepdims=True)
    grad_scores = (probs_wide * (grad_probs - inside)).astype(NARROW)
    gq = jnp.einsum("shqk,skhd->sqhd", grad_scores, kh, preferred_element_type=WIDE) * scale
    gk = jnp.einsum("shqk,sqhd->skhd", grad_scores, qh, preferred_element_type=WIDE) * scale
    gv = jnp.einsum("shqk,sqhd->skhd", probs, grad_context, preferred_element_type=WIDE)
    gq, gk, gv = (item.astype(NARROW).reshape(rows, width) for item in (gq, gk, gv))
    back_q = adapter_scale * mm_nt(gq, query_up)
    back_v = adapter_scale * mm_nt(gv, value_up)
    grad_input = (
        grad_first
        + mm_nt(gq, full_query)
        + mm_nt(gk, full_key)
        + mm_nt(gv, full_value)
        + mm_nt(back_q, query_down_frozen.astype(WIDE))
        + mm_nt(back_v, value_down_frozen.astype(WIDE))
    )
    grads = jnp.concatenate([mm_tn(u_q, gq), mm_tn(u_v, gv)], axis=0) * adapter_scale
    grads = lax.psum(grads, everyone)
    mine = query_up_trained.shape[1]
    grads = lax.dynamic_slice_in_dim(grads, place * mine, mine, axis=1)
    return (
        output.astype(NARROW),
        grad_input.astype(NARROW),
        grads[:ADAPTER_RANK],
        grads[ADAPTER_RANK:],
    )


IN_SPECS = (
    P(("dp", "tensor"), None),
    P(("dp", "tensor"), None),
    P("dp", "tensor"),
    P("dp", "tensor"),
    P("dp", "tensor"),
    P("tensor", "dp"),
    P("dp", "tensor"),
    P("tensor", "dp"),
    P("tensor"),
    P("tensor"),
    P(),
    P("tensor"),
    P(),
    P(),
    P(),
    P(None, "tensor"),
    P(None, "tensor"),
    P(),
    P(),
    P(),
    P(),
    P("dp"),
    P("dp"),
)
OUT_SPECS = (
    P(("dp", "tensor"), None),
    P(("dp", "tensor"), None),
    P(None, "tensor"),
    P(None, "tensor"),
)


def solution(mesh):
    return jax.shard_map(body, mesh=mesh, in_specs=IN_SPECS, out_specs=OUT_SPECS, check_vma=False)
```

profile of v0, /device:TPU:0, one launch (start us, length us, event | category | flops | bytes accessed | tf_op | source)
XLA Modules:
  0.0 609.4 jit_solution(543538263132884549)
XLA Ops:
  12.2 2.6 copy.141
  16.2 6.2 %all-gather.1 = bf16[4,192,8]{1,2,0:T(8,128)(2,1)S(1)} all-gather(bf16[1,192,8]{1,2,0:T(8,128)(2,1)S(1)} %bitcast.150), channel_id=1, replica_groups=mesh['dp'=8,'tensor'=4] {'tensor'}, dimensions={0}, use_global_device_ids=true | all-gather | bytes 15360 | tf_op jit(solution)/shard_map/all_gather | solution.py:91
  22.5 5.4 all-gather
  31.4 7.4 %all-reduce.2 = (f32[768]{0:T(1024)S(1)}, f32[768]{0:T(1024)S(1)}) all-reduce(f32[768]{0:T(1024)S(1)} %dynamic-update-slice.1, f32[768]{0:T(1024)S(1)} %dynamic-update-slice), channel_id=1, replica_groups=mesh['dp'=8,'tensor'=4] {'tensor'}, use_global_device_ids=true, to_apply=%add.1 | all-reduce | flops 1536 | bytes 12288
  38.8 5.2 all-gather.2
  46.4 22.4 %all-gather.14.cloned.1.call-done = bf16[3072,192]{1,0:T(8,128)(2,1)} async-done(((bf16[96,192]{1,0:T(8,128)(2,1)}), bf16[3072,192]{1,0:T(8,128)(2,1)}) %all-gather.14.cloned.1.call-update) | async-done | bytes 1179664 | tf_op jit(solution)/shard_map/all_gather | solution.py:72
  68.8 2.7 copy.172
  75.8 2.9 reshape.154
  78.7 47.1 %all-gather.12.cloned.1.call-done = bf16[3072,192]{1,0:T(8,128)(2,1)} async-done(((bf16[96,192]{1,0:T(8,128)(2,1)}), bf16[3072,192]{1,0:T(8,128)(2,1)}) %all-gather.12.cloned.1.call-update) | async-done | bytes 1179664 | tf_op jit(solution)/shard_map/all_gather | solution.py:72
  125.7 3.6 copy.171
  133.9 2.6 copy.127
  136.5 3.8 reshape.151
  140.4 42.3 %all-gather.10.cloned.1.call-done = bf16[3072,192]{1,0:T(8,128)(2,1)} async-done(((bf16[96,192]{1,0:T(8,128)(2,1)}), bf16[3072,192]{1,0:T(8,128)(2,1)}) %all-gather.10.cloned.1.call-update) | async-done | bytes 1179664 | tf_op jit(solution)/shard_map/all_gather | solution.py:72
  182.7 3.6 copy.170
  191.4 2.9 reshape.148
  194.4 14.7 %fusion.69 = (f32[2,12,512]{2,1,0:T(8,128)S(1)}, f32[2,12,512,512]{2,3,1,0:T(8,128)}) fusion(pred[2,512,512]{1,2,0:T(8,128)(4,1)} %and_or_fusion, bf16[2,512,12,64]{1,0,3,2:T(2,128)(2,1)S(1)} %reshape.154, bf16[2,512,12,64]{1,0,3,2:T(2,128)(2,1)} %reshape.151), kind=kOutput, calls=%fused_computation.113 | convolution fusion | flops 830472704 | bytes 28884992 | tf_op jit(solution)/shard_map/sub | solution.py:116
  209.1 10.2 %divide_convert_fusion = bf16[2,12,512,512]{2,3,1,0:T(8,128)(2,1)S(1)} fusion(f32[2,12,512,512]{2,3,1,0:T(8,128)} %get-tuple-element.30, f32[2,12,512]{2,1,0:T(8,128)S(1)} %get-tuple-element.29), kind=kLoop, calls=%fused_computation.5 | loop fusion | flops 12582912 | bytes 37797888 | tf_op jit(solution)/shard_map/convert_element_type | solution.py:117
  219.3 2.0 fusion.30
  221.3 2.5 copy-done.1
  227.0 12.4 %all-gather.16.cloned.1.call-done = bf16[3072,192]{1,0:T(8,128)(2,1)} async-done(((bf16[96,192]{1,0:T(8,128)(2,1)}), bf16[3072,192]{1,0:T(8,128)(2,1)}) %all-gather.16.cloned.1.call-update) | async-done | bytes 1179664 | tf_op jit(solution)/shard_map/all_gather | solution.py:72
  239.4 2.7 copy.173
  242.3 4.0 fusion.78
  246.7 58.1 %all-gather.20.cloned.1.call-done = bf16[3072,768]{1,0:T(8,128)(2,1)} async-done(((bf16[96,768]{1,0:T(8,128)(2,1)}), bf16[3072,768]{1,0:T(8,128)(2,1)}) %all-gather.20.cloned.1.call-update) | async-done | bytes 4718608 | tf_op jit(solution)/shard_map/all_gather | solution.py:72
  304.8 6.7 %copy.140 = bf16[768,4,768]{0,2,1:T(8,128)(2,1)} copy(bf16[768,4,768]{2,0,1:T(8,128)(2,1)} %bitcast.121) | data formatting | bytes 9437184 | tf_op jit(solution)/shard_map/transpose | solution.py:80
  311.4 58.6 %all-gather.18.cloned.1.call-done = bf16[3072,768]{1,0:T(8,128)(2,1)} async-done(((bf16[96,768]{1,0:T(8,128)(2,1)}), bf16[3072,768]{1,0:T(8,128)(2,1)}) %all-gather.18.cloned.1.call-update) | async-done | bytes 4718608 | tf_op jit(solution)/shard_map/all_gather | solution.py:72
  370.0 6.7 %copy.139 = bf16[768,4,768]{0,2,1:T(8,128)(2,1)} copy(bf16[768,4,768]{2,0,1:T(8,128)(2,1)} %bitcast.122) | data formatting | bytes 9437184 | tf_op jit(solution)/shard_map/transpose | solution.py:80
  376.7 36.2 %fusion.4 = (f32[1024,3072]{1,0:T(8,128)}, f32[1024,3072]{1,0:T(8,128)}) fusion(f32[3072]{0:T(1024)S(1)} %bitcast.147, bf16[768,3072]{0,1:T(8,128)(2,1)} %bitcast.125, f32[1024,768]{0,1:T(8,128)S(1)} %get-tuple-element.32, f32[768]{0:T(1024)S(1)} %copy-done.38, f32[768]{0:T(1024)S(1)} %copy-done.39, f32[1024]{0:T(1024)S(1)} %add_rsqrt_fusion.1, ...), kind=kOutput, calls=%fused_computation.10 | convolution fusion | flops 5033951232 | bytes 33056768 | tf_op jit(solution)/shard_map/dot_general | solution.py:32
  413.0 17.1 %fusion.79 = (f32[1024]{0:T(1024)S(1)}, f32[1024,768]{0,1:T(8,128)}) fusion(f32[768]{0:T(1024)S(1)} %copy-done.37, bf16[768,3072]{0,1:T(8,128)(2,1)} %bitcast.123, f32[1024,3072]{1,0:T(8,128)} %get-tuple-element.33, f32[1024,3072]{1,0:T(8,128)} %get-tuple-element.34, f32[3072]{0:T(1024)S(1)} %bitcast.148, f32[768]{0:T(1024)S(1)} %copy-done.38, ...), kind=kOutput, calls=%fused_computation.115 | convolution fusion | flops 4849925120 | bytes 36209664 | tf_op jit(solution)/shard_map/dot_general | solution.py:36
  430.1 2.4 multiply_reduce_fusion.2
  432.9 3.7 fusion.19
  436.6 25.4 %fusion.67 = (f32[1024]{0:T(1024)S(1)}, f32[1024]{0:T(1024)S(1)}, f32[1024,768]{0,1:T(8,128)}) fusion(f32[1024]{0:T(1024)S(1)} %add_rsqrt_fusion.1, f32[1024,768]{0,1:T(8,128)S(1)} %get-tuple-element.32, f32[1024]{0:T(1024)S(1)} %broadcast_multiply_fusion.5, f32[768]{0:T(1024)S(1)} %copy-done.39, bf16[768,3072]{0,1:T(8,128)(2,1)} %bitcast.126, ...), kind=kOutput, calls=%fused_computation.111 | convolution fusion | flops 9729734656 | bytes 45664256 | tf_op jit(solution)/shard_map/dot_general | solution.py:36
  462.0 5.5 convolution_convert_fusion.2
  467.5 2.8 copy.142
  470.3 2.9 reshape.162
  473.2 12.9 %fusion.1 = (f32[2,12,512]{2,1,0:T(8,128)S(1)}, f32[2,12,512,512]{2,3,1,0:T(8,128)}) fusion(bf16[2,12,512,512]{2,3,1,0:T(8,128)(2,1)} %copy-done.1, bf16[2,512,12,64]{1,0,3,2:T(2,128)(2,1)S(1)} %copy-done.4, bf16[2,512,12,64]{1,0,3,2:T(2,128)(2,1)S(1)} %reshape.162), kind=kOutput, calls=%fused_computation.3 | convolution fusion | flops 824168448 | bytes 40943616 | tf_op jit(solution)/shard_map/sqhd,skhd->shqk/dot_general | solution.py:135
  486.1 8.5 %fusion.31 = bf16[2,512,12,64]{1,3,2,0:T(8,128)(2,1)S(1)} fusion(bf16[2,12,512,512]{2,3,1,0:T(8,128)(2,1)} %copy-done.1, bf16[2,512,12,64]{1,0,3,2:T(2,128)(2,1)S(1)} %reshape.162), kind=kOutput, calls=%fused_computation.69 | convolution fusion | flops 806092800 | bytes 15728640 | tf_op jit(solution)/shard_map/shqk,sqhd->skhd/dot_general | solution.py:141
  494.6 17.1 %fusion.2 = bf16[2,12,512,512]{2,3,1,0:T(8,128)(2,1)S(1)} fusion(f32[2,12,512,512]{2,3,1,0:T(8,128)} %get-tuple-element.39, f32[2,12,512]{2,1,0:T(8,128)S(1)} %get-tuple-element.38, f32[2,12,512,512]{2,3,1,0:T(8,128)} %get-tuple-element.30, f32[2,12,512]{2,1,0:T(8,128)S(1)} %copy-done.18), kind=kLoop, calls=%fused_computation.4 | loop fusion | flops 37748736 | bytes 63012864 | tf_op jit(solution)/shard_map/convert_element_type | solution.py:138
  511.7 4.5 copy-done.2
  516.2 2.1 fusion.32
  518.3 9.6 %fusion.33 = bf16[2,512,12,64]{1,3,2,0:T(8,128)(2,1)} fusion(bf16[2,12,512,512]{2,3,1,0:T(8,128)(2,1)} %copy-done.2, bf16[2,512,12,64]{1,0,3,2:T(2,128)(2,1)S(1)} %copy-done.10), kind=kOutput, calls=%fused_computation.71 | convolution fusion | flops 806879232 | bytes 15728640 | tf_op jit(solution)/shard_map/shqk,sqhd->skhd/dot_general | solution.py:140
  530.0 2.5 fusion.52
  532.5 4.4 fusion.84
  538.9 3.2 fusion.86
  543.1 2.8 copy.159
  545.9 3.1 copy.151
  549.5 3.1 fusion.85
  552.6 7.4 %add_convert_fusion.2 = bf16[1024,768]{0,1:T(8,128)(2,1)S(1)} fusion(f32[1024,768]{0,1:T(8,128)} %fusion.52, f32[1024,768]{0,1:T(8,128)} %fusion.86, f32[1024,768]{0,1:T(8,128)} %fusion.85, f32[1024,768]{0,1:T(8,128)} %fusion.84, bf16[768,8]{0,1:T(8,128)(2,1)S(1)} %copy-done.28, bf16[1024,768]{0,1:T(8,128)(2,1)S(1)} %bitcast.113, ...), kind=kOutput, calls=%fused_computation.34 | convolution fusion | flops 34611200 | bytes 22061056 | tf_op jit(solution)/shard_map/dot_general | solution.py:36
  561.7 40.0 %psum.7 = f32[16,768]{1,0:T(8,128)S(1)} all-reduce(f32[16,768]{1,0:T(8,128)S(1)} %maximum_multiply_fusion), channel_id=1, replica_groups=mesh['dp'=8,'tensor'=4] {'tensor','dp'}, use_global_device_ids=true, to_apply=%region_11.12 | all-reduce | flops 12288 | bytes 98304 | tf_op jit(solution)/shard_map/psum | solution.py:154
  (143 shorter events, 37.6 us)
Async XLA Ops:
  7.2 38.2 %copy-start = (bf16[768,8]{0,1:T(8,128)(2,1)S(1)}, bf16[768,8]{0,1:T(8,128)(2,1)}, u32[]{:S(2)}) copy-start(bf16[768,8]{0,1:T(8,128)(2,1)} %param.36) | copy-start | bytes 36868
  7.2 7.6 %copy-start.33 = (f32[768]{0:T(1024)S(1)}, f32[768]{0:T(1024)}, u32[]{:S(2)}) copy-start(f32[768]{0:T(1024)} %param.34) | copy-start | bytes 9220
  7.2 9.0 %copy-start.31 = (bf16[8,192]{1,0:T(8,128)(2,1)S(1)}, bf16[8,192]{1,0:T(8,128)(2,1)}, u32[]{:S(2)}) copy-start(bf16[8,192]{1,0:T(8,128)(2,1)} %param.38) | copy-start | bytes 9220
  7.2 15.3 %copy-start.32 = (bf16[8,192]{1,0:T(8,128)(2,1)S(1)}, bf16[8,192]{1,0:T(8,128)(2,1)}, u32[]{:S(2)}) copy-start(bf16[8,192]{1,0:T(8,128)(2,1)} %param.39) | copy-start | bytes 9220
  7.2 20.8 %copy-start.5 = (bf16[1024,768]{1,0:T(8,128)(2,1)S(1)}, bf16[1024,768]{1,0:T(8,128)(2,1)}, u32[]{:S(2)}) copy-start(bf16[1024,768]{1,0:T(8,128)(2,1)} %param.23) | copy-start | bytes 4718596
  7.2 61.6 %all-gather.14.cloned.1.call-start = ((), (), s32[]{:S(2)}) async-start(), calls=%async_computation.2 | async-start | bytes 1622016 | tf_op jit(solution)/shard_map/all_gather | solution.py:72
  8.0 117.8 %all-gather.12.cloned.1.call-start = ((), (), s32[]{:S(2)}) async-start(), calls=%async_computation.1 | async-start | bytes 1622016 | tf_op jit(solution)/shard_map/all_gather | solution.py:72
  8.7 173.9 %all-gather.10.cloned.1.call-start = ((), (), s32[]{:S(2)}) async-start(), calls=%async_computation | async-start | bytes 1622016 | tf_op jit(solution)/shard_map/all_gather | solution.py:72
  9.4 230.0 %all-gather.16.cloned.1.call-start = ((), (), s32[]{:S(2)}) async-start(), calls=%async_computation.3 | async-start | bytes 1622016 | tf_op jit(solution)/shard_map/all_gather | solution.py:72
  11.0 293.8 %all-gather.20.cloned.1.call-start = ((), (), s32[]{:S(2)}) async-start(), calls=%async_computation.5 | async-start | bytes 4866048 | tf_op jit(solution)/shard_map/all_gather | solution.py:72
  11.6 358.4 %all-gather.18.cloned.1.call-start = ((), (), s32[]{:S(2)}) async-start(), calls=%async_computation.4 | async-start | bytes 4866048 | tf_op jit(solution)/shard_map/all_gather | solution.py:72
  12.2 17.5 %copy-start.40 = (u32[32]{0:T(128)S(1)}, u32[32]{0:T(128)}, u32[]{:S(2)}) copy-start(u32[32]{0:T(128)} %constant.103) | copy-start | bytes 388
  12.2 18.7 %copy-start.34 = (f32[192]{0:T(256)S(1)}, f32[192]{0:T(256)}, u32[]{:S(2)}) copy-start(f32[192]{0:T(256)} %param.31) | copy-start | bytes 2308
  12.2 18.9 %copy-start.35 = (f32[192]{0:T(256)S(1)}, f32[192]{0:T(256)}, u32[]{:S(2)}) copy-start(f32[192]{0:T(256)} %param.32) | copy-start | bytes 2308
  14.8 31.1 %copy-start.27 = (bf16[768,8]{0,1:T(8,128)(2,1)S(1)}, bf16[768,8]{0,1:T(8,128)(2,1)}, u32[]{:S(2)}) copy-start(bf16[768,8]{0,1:T(8,128)(2,1)} %param.37) | copy-start | bytes 36868
  22.5 109.6 %copy-start.25 = (bf16[768,8]{0,1:T(8,128)(2,1)}, bf16[768,8]{0,1:T(8,128)(2,1)S(1)}, u32[]{:S(2)}) copy-start(bf16[768,8]{0,1:T(8,128)(2,1)S(1)} %reshape.175) | copy-start | bytes 36868
  28.0 161.1 %copy-start.23 = (bf16[768,8]{0,1:T(8,128)(2,1)}, bf16[768,8]{0,1:T(8,128)(2,1)S(1)}, u32[]{:S(2)}) copy-start(bf16[768,8]{0,1:T(8,128)(2,1)S(1)} %reshape.173) | copy-start | bytes 36868
  45.9 86.3 %copy-start.19 = (bf16[1024,8]{0,1:T(8,128)(2,1)}, bf16[1024,8]{0,1:T(8,128)(2,1)S(1)}, u32[]{:S(2)}) copy-start(bf16[1024,8]{0,1:T(8,128)(2,1)S(1)} %convolution_convert_fusion.4) | copy-start | bytes 49156
  46.4 142.7 %copy-start.21 = (bf16[1024,8]{0,1:T(8,128)(2,1)}, bf16[1024,8]{0,1:T(8,128)(2,1)S(1)}, u32[]{:S(2)}) copy-start(bf16[1024,8]{0,1:T(8,128)(2,1)S(1)} %convolution_convert_fusion.5) | copy-start | bytes 49156
  71.7 1.0 copy-start.11
  78.6 115.7 %copy-start.8 = (bf16[2,512,12,64]{1,0,3,2:T(2,128)(2,1)}, bf16[2,512,12,64]{1,0,3,2:T(2,128)(2,1)S(1)}, u32[]{:S(2)}) copy-start(bf16[2,512,12,64]{1,0,3,2:T(2,128)(2,1)S(1)} %reshape.154) | copy-start | bytes 4718596
  130.7 1.4 copy-start.13
  187.6 1.4 copy-start.14
  194.3 25.0 %copy-start.3 = (bf16[2,512,12,64]{1,0,3,2:T(2,128)(2,1)}, bf16[2,512,12,64]{1,0,3,2:T(2,128)(2,1)S(1)}, u32[]{:S(2)}) copy-start(bf16[2,512,12,64]{1,0,3,2:T(2,128)(2,1)S(1)} %reshape.148) | copy-start | bytes 4718596
  209.1 10.2 %copy-start.17 = (f32[2,12,512]{2,1,0:T(8,128)}, f32[2,12,512]{2,1,0:T(8,128)S(1)}, u32[]{:S(2)}) copy-start(f32[2,12,512]{2,1,0:T(8,128)S(1)} %get-tuple-element.29) | copy-start | bytes 147460
  219.3 4.5 copy-start.1
  227.0 15.3 %copy-start.36 = (f32[768]{0:T(1024)S(1)}, f32[768]{0:T(1024)}, u32[]{:S(2)}) copy-start(f32[768]{0:T(1024)} %param.33) | copy-start | bytes 9220
  242.3 4.0 copy-start.16
  246.3 215.7 %copy-start.6 = (f32[1024,768]{0,1:T(8,128)}, f32[1024,768]{0,1:T(8,128)S(1)}, u32[]{:S(2)}) copy-start(f32[1024,768]{0,1:T(8,128)S(1)} %get-tuple-element.32) | copy-start | bytes 9437188
  370.0 6.7 %copy-start.38 = (f32[768]{0:T(1024)S(1)}, f32[768]{0:T(1024)}, u32[]{:S(2)}) copy-start(f32[768]{0:T(1024)} %param.41) | copy-start | bytes 9220
  370.0 6.7 %copy-start.39 = (f32[768]{0:T(1024)S(1)}, f32[768]{0:T(1024)}, u32[]{:S(2)}) copy-start(f32[768]{0:T(1024)} %param.40) | copy-start | bytes 9220
  376.7 36.2 %copy-start.37 = (f32[768]{0:T(1024)S(1)}, f32[768]{0:T(1024)}, u32[]{:S(2)}) copy-start(f32[768]{0:T(1024)} %param.35) | copy-start | bytes 9220
  430.1 2.8 copy-start.7
  430.1 2.8 copy-start.29
  430.1 2.8 copy-start.30
  467.5 5.7 copy-start.4
  486.1 8.5 %copy-start.18 = (f32[2,12,512]{2,1,0:T(8,128)S(1)}, f32[2,12,512]{2,1,0:T(8,128)}, u32[]{:S(2)}) copy-start(f32[2,12,512]{2,1,0:T(8,128)} %copy-done.17) | copy-start | bytes 147460
  494.6 21.6 %copy-start.9 = (bf16[2,512,12,64]{1,0,3,2:T(2,128)(2,1)S(1)}, bf16[2,512,12,64]{1,0,3,2:T(2,128)(2,1)}, u32[]{:S(2)}) copy-start(bf16[2,512,12,64]{1,0,3,2:T(2,128)(2,1)} %copy-done.8) | copy-start | bytes 4718596
  511.7 4.5 copy-start.2
  516.2 2.1 copy-start.10
  528.0 2.0 copy-start.26
  536.9 2.0 copy-start.15
  538.9 3.2 copy-start.22
  538.9 3.7 copy-start.20
  545.9 3.5 copy-start.12
  549.5 3.2 copy-start.24
  549.5 3.2 copy-start.28
Sparse Core Ops, SparseCore 0:
  11.0 57.8 all-gather.13
  71.7 53.9 all-gather.11
  128.6 53.9 all-gather.9
  185.4 53.9 all-gather.15
  242.2 62.5 all-gather.19
  307.5 62.4 all-gather.17
where the time goes:
time: 619 us; the launch traced here: 609 us
  waiting for transfers between devices  244 us (39%)
  matrix products  167 us (27%)
  local copies, waits for them, and re-layouts  82.2 us (13%)
  blocking collectives  64.1 us (10%)
  other arithmetic  35.9 us (6%)
  between operations  15.6 us (3%)
    all_gather x6, waiting for transfers between devices, spread(): return lax.all_gather(block, everyone, axis=0, tiled=True)  241 us
    dot_general x8, matrix products, mm_nt(): lax.dot_general(left, right, (((1,), (1,)), ((), ())), preferred_element_...  67 us
    dot_general x9, matrix products, mm(): return jnp.dot(left, right, preferred_element_type=WIDE)  49.5 us
    psum x1, blocking collectives, body(): grads = lax.psum(grads, everyone)  40 us
    unnamed x99, local copies, waits for them, and re-layouts  22.7 us
    convert_element_type x1, other arithmetic, body(): grad_scores = (probs_wide * (grad_probs - inside)).astype(NARROW)  17.1 us
    transpose x6, local copies, waits for them, and re-layouts, columns(): full.reshape(groups, width, block.shape[1]).transpose(1, 0, 2)  16.4 us
    sub x1, matrix products, body(): powers = jnp.exp(scores - highest)  14.7 us
  transfers between devices with their start and end apart: 6, of which 6 were waited for; matrix products, arithmetic and copies ran while one was open for 15% of the time, Pallas kernels for 0%

commit v1 on v0

--- a/solution.py
+++ b/solution.py
@@ -11,6 +11,12 @@
 NEG_FILL = -1e30
 WIDE = jnp.float32
 NARROW = jnp.bfloat16
+
+
+def gather_and_add(array, axis):
+    parts = lax.all_gather(array, axis, axis=0, tiled=False)
+    result = parts.sum(axis=0)
+    return result
 
 
 def layer_norm(rows, gain, shift):
@@ -151,7 +157,7 @@
         + mm_nt(back_v, value_down_frozen.astype(WIDE))
     )
     grads = jnp.concatenate([mm_tn(u_q, gq), mm_tn(u_v, gv)], axis=0) * adapter_scale
-    grads = lax.psum(grads, everyone)
+    grads = gather_and_add(grads, everyone)
     mine = query_up_trained.shape[1]
     grads = lax.dynamic_slice_in_dim(grads, place * mine, mine, axis=1)
     return (

time: 619 us -> 597 us (0.964)
  blocking collectives: 64.1 us -> 24.1 us
  waiting for transfers between devices: 244 us -> 263 us
    psum x1 -> x0, blocking collectives: 40 us -> none  [body(): grads = lax.psum(grads, everyone)]
    all_gather x0 -> x1, waiting for transfers between devices: none -> 19.3 us  [gather_and_add(): parts = lax.all_gather(array, axis, axis=0, tiled=False)]
    unnamed x99 -> x103, local copies, waits for them, and re-layouts: 22.7 us -> 20.5 us
  transfers between devices with their start and end apart: 6 -> 7, of which waited for: 6 -> 7; matrix products, arithmetic and copies ran while one was open for 15% -> 21% of each run, Pallas kernels for 0% -> 0%
where the time goes in v1:
time: 597 us; the launch traced here: 588 us
  waiting for transfers between devices  263 us (44%)
  matrix products  168 us (28%)
  local copies, waits for them, and re-layouts  78.5 us (13%)
  other arithmetic  38 us (6%)
  blocking collectives  24.1 us (4%)
  between operations  15.6 us (3%)
    all_gather x6, waiting for transfers between devices, spread(): return lax.all_gather(block, everyone, axis=0, tiled=True)  241 us
    dot_general x8, matrix products, mm_nt(): lax.dot_general(left, right, (((1,), (1,)), ((), ())), preferred_element_...  67.4 us
    dot_general x9, matrix products, mm(): return jnp.dot(left, right, preferred_element_type=WIDE)  49.5 us
    unnamed x103, local copies, waits for them, and re-layouts  20.5 us
    all_gather x1, waiting for transfers between devices, gather_and_add(): parts = lax.all_gather(array, axis, axis=0, tiled=False)  19.3 us
    convert_element_type x1, other arithmetic, body(): grad_scores = (probs_wide * (grad_probs - inside)).astype(NARROW)  17.1 us
    transpose x6, local copies, waits for them, and re-layouts, columns(): full.reshape(groups, width, block.shape[1]).transpose(1, 0, 2)  16.3 us
    sub x1, matrix products, body(): powers = jnp.exp(scores - highest)  14.7 us
  transfers between devices with their start and end apart: 7, of which 7 were waited for; matrix products, arithmetic and copies ran while one was open for 21% of the time, Pallas kernels for 0%

profile of v1, /device:TPU:0, one launch (start us, length us, event | category | flops | bytes accessed | tf_op | source)
XLA Modules:
  0.0 588.1 jit_solution(11366298508995397647)
XLA Ops:
  12.3 2.6 copy.141
  16.3 6.2 %all-gather.1 = bf16[4,192,8]{1,2,0:T(8,128)(2,1)S(1)} all-gather(bf16[1,192,8]{1,2,0:T(8,128)(2,1)S(1)} %bitcast.154), channel_id=1, replica_groups=mesh['dp'=8,'tensor'=4] {'tensor'}, dimensions={0}, use_global_device_ids=true | all-gather | bytes 15360 | tf_op jit(solution)/shard_map/all_gather | solution.py:97
  22.6 5.4 all-gather
  28.1 1.6 copy.119
  31.4 7.4 %all-reduce.2 = (f32[768]{0:T(1024)S(1)}, f32[768]{0:T(1024)S(1)}) all-reduce(f32[768]{0:T(1024)S(1)} %dynamic-update-slice.1, f32[768]{0:T(1024)S(1)} %dynamic-update-slice), channel_id=1, replica_groups=mesh['dp'=8,'tensor'=4] {'tensor'}, use_global_device_ids=true, to_apply=%add.1 | all-reduce | flops 1536 | bytes 12288
  38.8 5.2 all-gather.2
  46.4 22.4 %all-gather.15.cloned.1.call-done = bf16[3072,192]{1,0:T(8,128)(2,1)} async-done(((bf16[96,192]{1,0:T(8,128)(2,1)}), bf16[3072,192]{1,0:T(8,128)(2,1)}) %all-gather.15.cloned.1.call-update) | async-done | bytes 1179664 | tf_op jit(solution)/shard_map/all_gather | solution.py:78
  68.8 2.7 copy.172
  75.8 2.9 reshape.183
  78.7 47.1 %all-gather.13.cloned.1.call-done = bf16[3072,192]{1,0:T(8,128)(2,1)} async-done(((bf16[96,192]{1,0:T(8,128)(2,1)}), bf16[3072,192]{1,0:T(8,128)(2,1)}) %all-gather.13.cloned.1.call-update) | async-done | bytes 1179664 | tf_op jit(solution)/shard_map/all_gather | solution.py:78
  125.7 3.6 copy.171
  132.2 1.8 add_convert_fusion.4
  134.0 2.6 copy.127
  136.5 3.9 reshape.180
  140.4 42.2 %all-gather.11.cloned.1.call-done = bf16[3072,192]{1,0:T(8,128)(2,1)} async-done(((bf16[96,192]{1,0:T(8,128)(2,1)}), bf16[3072,192]{1,0:T(8,128)(2,1)}) %all-gather.11.cloned.1.call-update) | async-done | bytes 1179664 | tf_op jit(solution)/shard_map/all_gather | solution.py:78
  182.7 3.6 copy.170
  191.4 2.9 reshape.177
  194.3 14.7 %fusion.69 = (f32[2,12,512]{2,1,0:T(8,128)S(1)}, f32[2,12,512,512]{2,3,1,0:T(8,128)}) fusion(pred[2,512,512]{1,2,0:T(8,128)(4,1)} %and_or_fusion, bf16[2,512,12,64]{1,0,3,2:T(2,128)(2,1)S(1)} %reshape.183, bf16[2,512,12,64]{1,0,3,2:T(2,128)(2,1)} %reshape.180), kind=kOutput, calls=%fused_computation.115 | convolution fusion | flops 830472704 | bytes 28884992 | tf_op jit(solution)/shard_map/sub | solution.py:122
  209.0 10.2 %divide_convert_fusion = bf16[2,12,512,512]{2,3,1,0:T(8,128)(2,1)S(1)} fusion(f32[2,12,512,512]{2,3,1,0:T(8,128)} %get-tuple-element.30, f32[2,12,512]{2,1,0:T(8,128)S(1)} %get-tuple-element.29), kind=kLoop, calls=%fused_computation.5 | loop fusion | flops 12582912 | bytes 37797888 | tf_op jit(solution)/shard_map/convert_element_type | solution.py:123
  219.2 2.0 fusion.30
  221.2 2.5 copy-done.1
  226.9 12.5 %all-gather.17.cloned.1.call-done = bf16[3072,192]{1,0:T(8,128)(2,1)} async-done(((bf16[96,192]{1,0:T(8,128)(2,1)}), bf16[3072,192]{1,0:T(8,128)(2,1)}) %all-gather.17.cloned.1.call-update) | async-done | bytes 1179664 | tf_op jit(solution)/shard_map/all_gather | solution.py:78
  239.4 2.7 copy.173
  242.3 4.0 fusion.78
  246.7 58.1 %all-gather.21.cloned.1.call-done = bf16[3072,768]{1,0:T(8,128)(2,1)} async-done(((bf16[96,768]{1,0:T(8,128)(2,1)}), bf16[3072,768]{1,0:T(8,128)(2,1)}) %all-gather.21.cloned.1.call-update) | async-done | bytes 4718608 | tf_op jit(solution)/shard_map/all_gather | solution.py:78
  304.8 6.7 %copy.140 = bf16[768,4,768]{0,2,1:T(8,128)(2,1)} copy(bf16[768,4,768]{2,0,1:T(8,128)(2,1)} %bitcast.125) | data formatting | bytes 9437184 | tf_op jit(solution)/shard_map/transpose | solution.py:86
  311.4 58.6 %all-gather.19.cloned.1.call-done = bf16[3072,768]{1,0:T(8,128)(2,1)} async-done(((bf16[96,768]{1,0:T(8,128)(2,1)}), bf16[3072,768]{1,0:T(8,128)(2,1)}) %all-gather.19.cloned.1.call-update) | async-done | bytes 4718608 | tf_op jit(solution)/shard_map/all_gather | solution.py:78
  370.1 6.6 %copy.139 = bf16[768,4,768]{0,2,1:T(8,128)(2,1)} copy(bf16[768,4,768]{2,0,1:T(8,128)(2,1)} %bitcast.126) | data formatting | bytes 9437184 | tf_op jit(solution)/shard_map/transpose | solution.py:86
  376.7 36.2 %fusion.4 = (f32[1024,3072]{1,0:T(8,128)}, f32[1024,3072]{1,0:T(8,128)}) fusion(f32[3072]{0:T(1024)S(1)} %bitcast.151, bf16[768,3072]{0,1:T(8,128)(2,1)} %bitcast.129, f32[1024,768]{0,1:T(8,128)S(1)} %get-tuple-element.32, f32[768]{0:T(1024)S(1)} %copy-done.40, f32[768]{0:T(1024)S(1)} %copy-done.41, f32[1024]{0:T(1024)S(1)} %add_rsqrt_fusion.1, ...), kind=kOutput, calls=%fused_computation.10 | convolution fusion | flops 5033951232 | bytes 33056768 | tf_op jit(solution)/shard_map/dot_general | solution.py:38
  413.0 17.1 %fusion.79 = (f32[1024]{0:T(1024)S(1)}, f32[1024,768]{0,1:T(8,128)}) fusion(f32[768]{0:T(1024)S(1)} %copy-done.39, bf16[768,3072]{0,1:T(8,128)(2,1)} %bitcast.127, f32[1024,3072]{1,0:T(8,128)} %get-tuple-element.33, f32[1024,3072]{1,0:T(8,128)} %get-tuple-element.34, f32[3072]{0:T(1024)S(1)} %bitcast.152, f32[768]{0:T(1024)S(1)} %copy-done.40, ...), kind=kOutput, calls=%fused_computation.117 | convolution fusion | flops 4849925120 | bytes 36209664 | tf_op jit(solution)/shard_map/dot_general | solution.py:42
  430.0 2.4 multiply_reduce_fusion.2
  432.9 3.6 fusion.19
  436.5 25.4 %fusion.67 = (f32[1024]{0:T(1024)S(1)}, f32[1024]{0:T(1024)S(1)}, f32[1024,768]{0,1:T(8,128)}) fusion(f32[1024]{0:T(1024)S(1)} %add_rsqrt_fusion.1, f32[1024,768]{0,1:T(8,128)S(1)} %get-tuple-element.32, f32[1024]{0:T(1024)S(1)} %broadcast_multiply_fusion.5, f32[768]{0:T(1024)S(1)} %copy-done.41, bf16[768,3072]{0,1:T(8,128)(2,1)} %bitcast.130, ...), kind=kOutput, calls=%fused_computation.113 | convolution fusion | flops 9729734656 | bytes 45664256 | tf_op jit(solution)/shard_map/dot_general | solution.py:42
  461.9 5.5 convolution_convert_fusion.2
  467.5 2.8 copy.142
  470.3 2.9 reshape.191
  473.2 12.9 %fusion.1 = (f32[2,12,512]{2,1,0:T(8,128)S(1)}, f32[2,12,512,512]{2,3,1,0:T(8,128)}) fusion(bf16[2,12,512,512]{2,3,1,0:T(8,128)(2,1)} %copy-done.1, bf16[2,512,12,64]{1,0,3,2:T(2,128)(2,1)S(1)} %copy-done.4, bf16[2,512,12,64]{1,0,3,2:T(2,128)(2,1)S(1)} %reshape.191), kind=kOutput, calls=%fused_computation.3 | convolution fusion | flops 824168448 | bytes 40943616 | tf_op jit(solution)/shard_map/sqhd,skhd->shqk/dot_general | solution.py:141
  486.0 9.7 %fusion.31 = bf16[2,512,12,64]{1,3,2,0:T(8,128)(2,1)} fusion(bf16[2,12,512,512]{2,3,1,0:T(8,128)(2,1)} %copy-done.1, bf16[2,512,12,64]{1,0,3,2:T(2,128)(2,1)S(1)} %reshape.191), kind=kOutput, calls=%fused_computation.69 | convolution fusion | flops 806092800 | bytes 15728640 | tf_op jit(solution)/shard_map/shqk,sqhd->skhd/dot_general | solution.py:147
  497.3 17.1 %fusion.2 = bf16[2,12,512,512]{2,3,1,0:T(8,128)(2,1)S(1)} fusion(f32[2,12,512,512]{2,3,1,0:T(8,128)} %get-tuple-element.39, f32[2,12,512]{2,1,0:T(8,128)S(1)} %get-tuple-element.38, f32[2,12,512,512]{2,3,1,0:T(8,128)} %get-tuple-element.30, f32[2,12,512]{2,1,0:T(8,128)S(1)} %copy-done.20), kind=kLoop, calls=%fused_computation.4 | loop fusion | flops 37748736 | bytes 63012864 | tf_op jit(solution)/shard_map/convert_element_type | solution.py:144
  514.5 2.1 fusion.32
  516.6 2.4 copy-done.2
  524.8 9.0 %fusion.33 = bf16[2,512,12,64]{1,3,2,0:T(8,128)(2,1)S(1)} fusion(bf16[2,12,512,512]{2,3,1,0:T(8,128)(2,1)} %copy-done.2, bf16[2,512,12,64]{1,0,3,2:T(2,128)(2,1)} %reshape.180), kind=kOutput, calls=%fused_computation.71 | convolution fusion | flops 806879232 | bytes 15728640 | tf_op jit(solution)/shard_map/shqk,sqhd->skhd/dot_general | solution.py:146
  537.0 2.5 fusion.52
  539.4 4.7 fusion.86
  544.2 3.2 fusion.84
  547.4 3.1 fusion.85
  550.5 7.4 %add_convert_fusion.2 = bf16[1024,768]{0,1:T(8,128)(2,1)S(1)} fusion(f32[1024,768]{0,1:T(8,128)} %fusion.52, f32[1024,768]{0,1:T(8,128)} %fusion.86, f32[1024,768]{0,1:T(8,128)} %fusion.85, f32[1024,768]{0,1:T(8,128)} %fusion.84, bf16[768,8]{0,1:T(8,128)(2,1)S(1)} %copy-done.30, bf16[1024,768]{0,1:T(8,128)(2,1)S(1)} %bitcast.117, ...), kind=kOutput, calls=%fused_computation.34 | convolution fusion | flops 34611200 | bytes 22061056 | tf_op jit(solution)/shard_map/dot_general | solution.py:42
  559.5 19.3 %all-gather.23.cloned.1.call-done = f32[32,16,768]{2,1,0:T(8,128)} async-done(((f32[1,16,768]{2,1,0:T(8,128)}), f32[32,16,768]{2,1,0:T(8,128)}) %all-gather.23.cloned.1.call-update) | async-done | bytes 1572880 | tf_op jit(solution)/shard_map/all_gather | solution.py:17
  (150 shorter events, 40.6 us)
Async XLA Ops:
  7.2 38.2 %copy-start = (bf16[768,8]{0,1:T(8,128)(2,1)S(1)}, bf16[768,8]{0,1:T(8,128)(2,1)}, u32[]{:S(2)}) copy-start(bf16[768,8]{0,1:T(8,128)(2,1)} %param.36) | copy-start | bytes 36868
  7.2 7.7 %copy-start.35 = (f32[768]{0:T(1024)S(1)}, f32[768]{0:T(1024)}, u32[]{:S(2)}) copy-start(f32[768]{0:T(1024)} %param.34) | copy-start | bytes 9220
  7.2 9.1 %copy-start.33 = (bf16[8,192]{1,0:T(8,128)(2,1)S(1)}, bf16[8,192]{1,0:T(8,128)(2,1)}, u32[]{:S(2)}) copy-start(bf16[8,192]{1,0:T(8,128)(2,1)} %param.38) | copy-start | bytes 9220
  7.2 15.4 %copy-start.34 = (bf16[8,192]{1,0:T(8,128)(2,1)S(1)}, bf16[8,192]{1,0:T(8,128)(2,1)}, u32[]{:S(2)}) copy-start(bf16[8,192]{1,0:T(8,128)(2,1)} %param.39) | copy-start | bytes 9220
  7.2 20.8 %copy-start.5 = (bf16[1024,768]{1,0:T(8,128)(2,1)S(1)}, bf16[1024,768]{1,0:T(8,128)(2,1)}, u32[]{:S(2)}) copy-start(bf16[1024,768]{1,0:T(8,128)(2,1)} %param.23) | copy-start | bytes 4718596
  7.2 61.6 %all-gather.15.cloned.1.call-start = ((), (), s32[]{:S(2)}) async-start(), calls=%async_computation.2 | async-start | bytes 1622016 | tf_op jit(solution)/shard_map/all_gather | solution.py:78
  8.0 117.8 %all-gather.13.cloned.1.call-start = ((), (), s32[]{:S(2)}) async-start(), calls=%async_computation.1 | async-start | bytes 1622016 | tf_op jit(solution)/shard_map/all_gather | solution.py:78
  8.7 174.0 %all-gather.11.cloned.1.call-start = ((), (), s32[]{:S(2)}) async-start(), calls=%async_computation | async-start | bytes 1622016 | tf_op jit(solution)/shard_map/all_gather | solution.py:78
  9.4 230.0 %all-gather.17.cloned.1.call-start = ((), (), s32[]{:S(2)}) async-start(), calls=%async_computation.3 | async-start | bytes 1622016 | tf_op jit(solution)/shard_map/all_gather | solution.py:78
  11.0 293.7 %all-gather.21.cloned.1.call-start = ((), (), s32[]{:S(2)}) async-start(), calls=%async_computation.5 | async-start | bytes 4866048 | tf_op jit(solution)/shard_map/all_gather | solution.py:78
  11.6 358.4 %all-gather.19.cloned.1.call-start = ((), (), s32[]{:S(2)}) async-start(), calls=%async_computation.4 | async-start | bytes 4866048 | tf_op jit(solution)/shard_map/all_gather | solution.py:78
  12.2 566.7 %all-gather.23.cloned.1.call-start = ((), (), s32[]{:S(2)}) async-start(), calls=%async_computation.6 | async-start | bytes 1622016 | tf_op jit(solution)/shard_map/all_gather | solution.py:17
  12.2 17.5 %copy-start.42 = (u32[32]{0:T(128)S(1)}, u32[32]{0:T(128)}, u32[]{:S(2)}) copy-start(u32[32]{0:T(128)} %constant.103) | copy-start | bytes 388
  12.3 18.7 %copy-start.36 = (f32[192]{0:T(256)S(1)}, f32[192]{0:T(256)}, u32[]{:S(2)}) copy-start(f32[192]{0:T(256)} %param.31) | copy-start | bytes 2308
  12.3 18.9 %copy-start.37 = (f32[192]{0:T(256)S(1)}, f32[192]{0:T(256)}, u32[]{:S(2)}) copy-start(f32[192]{0:T(256)} %param.32) | copy-start | bytes 2308
  14.9 31.0 %copy-start.29 = (bf16[768,8]{0,1:T(8,128)(2,1)S(1)}, bf16[768,8]{0,1:T(8,128)(2,1)}, u32[]{:S(2)}) copy-start(bf16[768,8]{0,1:T(8,128)(2,1)} %param.37) | copy-start | bytes 36868
  22.6 109.6 %copy-start.25 = (bf16[768,8]{0,1:T(8,128)(2,1)}, bf16[768,8]{0,1:T(8,128)(2,1)S(1)}, u32[]{:S(2)}) copy-start(bf16[768,8]{0,1:T(8,128)(2,1)S(1)} %reshape.204) | copy-start | bytes 36868
  28.1 161.0 %copy-start.27 = (bf16[768,8]{0,1:T(8,128)(2,1)}, bf16[768,8]{0,1:T(8,128)(2,1)S(1)}, u32[]{:S(2)}) copy-start(bf16[768,8]{0,1:T(8,128)(2,1)S(1)} %reshape.202) | copy-start | bytes 36868
  45.9 86.3 %copy-start.21 = (bf16[1024,8]{0,1:T(8,128)(2,1)}, bf16[1024,8]{0,1:T(8,128)(2,1)S(1)}, u32[]{:S(2)}) copy-start(bf16[1024,8]{0,1:T(8,128)(2,1)S(1)} %convolution_convert_fusion.4) | copy-start | bytes 49156
  46.4 142.6 %copy-start.23 = (bf16[1024,8]{0,1:T(8,128)(2,1)}, bf16[1024,8]{0,1:T(8,128)(2,1)S(1)}, u32[]{:S(2)}) copy-start(bf16[1024,8]{0,1:T(8,128)(2,1)S(1)} %convolution_convert_fusion.5) | copy-start | bytes 49156
  78.7 115.6 %copy-start.8 = (bf16[2,512,12,64]{1,0,3,2:T(2,128)(2,1)}, bf16[2,512,12,64]{1,0,3,2:T(2,128)(2,1)S(1)}, u32[]{:S(2)}) copy-start(bf16[2,512,12,64]{1,0,3,2:T(2,128)(2,1)S(1)} %reshape.183) | copy-start | bytes 4718596
  130.7 1.4 copy-start.15
  187.6 1.4 copy-start.17
  194.3 25.0 %copy-start.3 = (bf16[2,512,12,64]{1,0,3,2:T(2,128)(2,1)}, bf16[2,512,12,64]{1,0,3,2:T(2,128)(2,1)S(1)}, u32[]{:S(2)}) copy-start(bf16[2,512,12,64]{1,0,3,2:T(2,128)(2,1)S(1)} %reshape.177) | copy-start | bytes 4718596
  209.0 10.2 %copy-start.19 = (f32[2,12,512]{2,1,0:T(8,128)}, f32[2,12,512]{2,1,0:T(8,128)S(1)}, u32[]{:S(2)}) copy-start(f32[2,12,512]{2,1,0:T(8,128)S(1)} %get-tuple-element.29) | copy-start | bytes 147460
  219.2 4.5 copy-start.1
  226.9 15.4 %copy-start.38 = (f32[768]{0:T(1024)S(1)}, f32[768]{0:T(1024)}, u32[]{:S(2)}) copy-start(f32[768]{0:T(1024)} %param.33) | copy-start | bytes 9220
  242.3 4.0 copy-start.18
  246.3 215.6 %copy-start.6 = (f32[1024,768]{0,1:T(8,128)}, f32[1024,768]{0,1:T(8,128)S(1)}, u32[]{:S(2)}) copy-start(f32[1024,768]{0,1:T(8,128)S(1)} %get-tuple-element.32) | copy-start | bytes 9437188
  370.1 6.7 %copy-start.40 = (f32[768]{0:T(1024)S(1)}, f32[768]{0:T(1024)}, u32[]{:S(2)}) copy-start(f32[768]{0:T(1024)} %param.41) | copy-start | bytes 9220
  370.1 6.7 %copy-start.41 = (f32[768]{0:T(1024)S(1)}, f32[768]{0:T(1024)}, u32[]{:S(2)}) copy-start(f32[768]{0:T(1024)} %param.40) | copy-start | bytes 9220
  376.7 36.2 %copy-start.39 = (f32[768]{0:T(1024)S(1)}, f32[768]{0:T(1024)}, u32[]{:S(2)}) copy-start(f32[768]{0:T(1024)} %param.35) | copy-start | bytes 9220
  430.0 2.8 copy-start.7
  430.0 2.8 copy-start.31
  430.0 2.8 copy-start.32
  467.5 5.7 copy-start.4
  486.0 9.7 %copy-start.10 = (bf16[1024,768]{0,1:T(8,128)(2,1)S(1)}, bf16[1024,768]{0,1:T(8,128)(2,1)}, u32[]{:S(2)}) copy-start(bf16[1024,768]{0,1:T(8,128)(2,1)} %get-tuple-element.26) | copy-start | bytes 4718596
  495.8 1.6 copy-start.20
  497.3 17.1 %copy-start.9 = (bf16[2,512,12,64]{1,0,3,2:T(2,128)(2,1)S(1)}, bf16[2,512,12,64]{1,0,3,2:T(2,128)(2,1)}, u32[]{:S(2)}) copy-start(bf16[2,512,12,64]{1,0,3,2:T(2,128)(2,1)} %copy-done.8) | copy-start | bytes 4718596
  514.5 4.5 copy-start.2
  519.0 2.0 copy-start.11
  521.1 2.1 copy-start.24
  533.8 3.2 copy-start.26
  539.4 4.7 copy-start.16
  544.2 3.2 copy-start.12
  544.2 3.2 copy-start.14
  547.4 3.2 copy-start.28
  547.4 3.2 copy-start.30
  (2 other events, 2.0 us)
Sparse Core Ops, SparseCore 0:
  11.0 57.8 all-gather.14
  71.7 53.9 all-gather.12
  128.7 53.9 all-gather.10
  185.4 53.9 all-gather.16
  242.2 62.5 all-gather.20
  307.5 62.4 all-gather.18
  524.9 53.8 all-gather.22
